TPU v7x, 32 devices: a whole 2x2x4 slice. The times are simulated.
32 devices in a mesh: img: 8 (over y, x, core), head: 4 (over z).
Axes of the slice: x: 2, y: 2, z: 4, core: 2. Of those that a mesh axis runs over, the one named last changes fastest.
Arguments:
- tokens: bfloat16 [40, 256, 768], P('img'), may hold values from -6 to 6
- mask_embed: float32 [768], replicated, may hold values from -6 to 6
- norm_gains: float32 [2, 768], replicated, may hold values from 0.1 to 1.9
- norm_shifts: float32 [2, 768], replicated, may hold values from -4 to 4
- qkv_weight: bfloat16 [3, 768, 768], P(None, None, 'head'), may hold values from -0.3125 to 0.3125
- qv_bias: float32 [2, 768], P(None, 'head'), may hold values from -4 to 4
- out_weight: bfloat16 [768, 768], P('head'), may hold values from -0.4375 to 0.4375
- output_biases: float32 [2, 768], replicated, may hold values from -4 to 4
- up_weight: bfloat16 [768, 3072], P(None, 'head'), may hold values from -0.21875 to 0.21875
- up_bias: float32 [3072], P('head'), may hold values from -4 to 4
- down_weight: bfloat16 [3072, 768], P('head'), may hold values from -0.109375 to 0.109375
- counts: int32 [40], P('img'), may hold values from 1 to 256, as said below
- token_ranks: int32 [40, 256], P('img'), may hold values from 0 to 255, each once within a row
- cotangent: bfloat16 [40, 256, 768], P('img'), may hold values from -6 to 6
Outputs:
- out: bfloat16 [40, 256, 768], P('img')
- tokens_grad: float32 [40, 256, 768], P('img')
- mask_embed_grad: float32 [768], replicated
- norm_gains_grad: float32 [2, 768], replicated
- norm_shifts_grad: float32 [2, 768], replicated
- qkv_weight_grad: float32 [3, 768, 768], P(None, None, 'head')
- qv_bias_grad: float32 [2, 768], P(None, 'head')
- out_weight_grad: float32 [768, 768], P('head')
- output_biases_grad: float32 [2, 768], replicated
- up_weight_grad: float32 [768, 3072], P(None, 'head')
- up_bias_grad: float32 [3072], P('head')
- down_weight_grad: float32 [3072, 768], P('head')
Inputs may be any that keep to these rules, and one draw needn't show every extreme that they name: `counts`: each image's count follows the cosine masking plan over 256 tokens. `token_ranks`: each image's row is a permutation of 0 to 255.
All inputs are finite; a program needn't handle non-finite values.
Results may differ from a plain program's by a relative error of at most 0.012.
The roundings to bfloat16 on the way count: a program that leaves them out, or rounds other values in their place, can miss the bound.
Values sent between devices are 32-bit elements; how exact they have to be, the bound alone decides.
No kernel may reach another device: no remote copies, remote signals or barrier semaphores. Data moves between devices by JAX's collectives and lax.ppermute only.
A program may use at most 128 MiB of HBM per device.

v0:
```python
from functools import partial
import jax
import jax.numpy as jnp
from jax import lax
from jax.sharding import PartitionSpec as P

HEAD_DIM = 48
norm_eps = 1e-06


def contract_rows(left, right):
    return lax.dot_general(
        left, right, (((0,), (0,)), ((), ())), preferred_element_type=jnp.float32
    )


def times_transposed(left, right):
    return lax.dot_general(
        left, right, (((1,), (1,)), ((), ())), preferred_element_type=jnp.float32
    )


def normalize(values, scaling, offset):
    center = values - jnp.mean(values, axis=-1, keepdims=True)
    inverse = lax.rsqrt(jnp.mean(center * center, axis=-1, keepdims=True) + norm_eps)
    normal = center * inverse
    return (normal * scaling + offset, normal, inverse)


def normalize_back(upstream, normal, inverse, scaling):
    scaled = upstream * scaling
    inner = (
        scaled
        - jnp.mean(scaled, axis=-1, keepdims=True)
        - normal * jnp.mean(scaled * normal, axis=-1, keepdims=True)
    )
    return (inverse * inner, jnp.sum(upstream * normal, axis=0), jnp.sum(upstream, axis=0))


def forward(start, params, images, seq_len):
    (
        norm_gains,
        norm_shifts,
        qkv_weight,
        qv_bias,
        out_weight,
        output_biases,
        up_weight,
        up_bias,
        down_weight,
    ) = params
    local_width = qkv_weight.shape[2]
    head_shape = (images, seq_len, local_width // HEAD_DIM, HEAD_DIM)
    score_scale = HEAD_DIM ** (-0.5)
    attn_normed, attn_normal, attn_inverse = normalize(start, norm_gains[0], norm_shifts[0])
    attn_normed = attn_normed.astype(jnp.bfloat16)
    bias_rows = jnp.stack([qv_bias[0], jnp.zeros_like(qv_bias[0]), qv_bias[1]])
    projected = jnp.einsum(
        "td,ndc->ntc", attn_normed, qkv_weight, preferred_element_type=jnp.float32
    )
    projected = (projected + bias_rows[:, None, :]).astype(jnp.bfloat16)
    scores = (
        jnp.einsum(
            "bqhd,bkhd->bhqk",
            projected[0].reshape(head_shape),
            projected[1].reshape(head_shape),
            preferred_element_type=jnp.float32,
        )
        * score_scale
    )
    row_max = jnp.max(scores, axis=-1, keepdims=True)
    exponent = jnp.exp(scores - row_max)
    row_total = jnp.sum(exponent, axis=-1, keepdims=True)
    attn_probs = (exponent / row_total).astype(jnp.bfloat16)
    log_total = row_max + jnp.log(row_total)
    mixed = jnp.einsum(
        "bhqk,bkhd->bqhd",
        attn_probs,
        projected[2].reshape(head_shape),
        preferred_element_type=jnp.float32,
    )
    mixed = mixed.reshape(start.shape[0], local_width).astype(jnp.bfloat16)
    attended = lax.psum(jnp.dot(mixed, out_weight, preferred_element_type=jnp.float32), "head")
    after_attn = start + attended + output_biases[0]
    mlp_normed, mlp_normal, mlp_inverse = normalize(after_attn, norm_gains[1], norm_shifts[1])
    mlp_normed = mlp_normed.astype(jnp.bfloat16)
    pre_act = jnp.dot(mlp_normed, up_weight, preferred_element_type=jnp.float32) + up_bias
    activated = jax.nn.gelu(pre_act, approximate=True).astype(jnp.bfloat16)
    branch = lax.psum(jnp.dot(activated, down_weight, preferred_element_type=jnp.float32), "head")
    after_mlp = after_attn + branch + output_biases[1]
    saved = (
        attn_normal,
        attn_inverse,
        attn_normed,
        projected,
        log_total,
        mixed,
        mlp_normal,
        mlp_inverse,
        mlp_normed,
        pre_act,
        activated,
    )
    return (after_mlp, saved)


def per_device(
    tokens,
    mask_embed,
    norm_gains,
    norm_shifts,
    qkv_weight,
    qv_bias,
    out_weight,
    output_biases,
    up_weight,
    up_bias,
    down_weight,
    counts,
    token_ranks,
    cotangent,
):
    images, seq_len, model_width = tokens.shape
    row_count = images * seq_len
    local_width = qkv_weight.shape[2]
    head_shape = (images, seq_len, local_width // HEAD_DIM, HEAD_DIM)
    score_scale = HEAD_DIM ** (-0.5)
    local_count = jnp.sum(counts.astype(jnp.float32))
    masked_sum = lax.psum(local_count, "img")
    is_masked = (token_ranks < counts[:, None]).reshape(row_count, 1)
    mask_col = is_masked.astype(jnp.float32)
    start = jnp.where(
        is_masked, mask_embed[None, :], tokens.reshape(row_count, model_width).astype(jnp.float32)
    )
    params = (
        norm_gains,
        norm_shifts,
        qkv_weight,
        qv_bias,
        out_weight,
        output_biases,
        up_weight,
        up_bias,
        down_weight,
    )
    result, saved = forward(start, params, images, seq_len)
    again = lax.optimization_barrier((start, result))[0]
    unused, saved = forward(again, params, images, seq_len)
    (
        attn_normal,
        attn_inverse,
        attn_normed,
        projected,
        log_total,
        mixed,
        mlp_normal,
        mlp_inverse,
        mlp_normed,
        pre_act,
        activated,
    ) = saved
    signal = cotangent.reshape(row_count, model_width).astype(jnp.float32) * mask_col
    signal_low = signal.astype(jnp.bfloat16)
    down_bias_raw = jnp.sum(signal, axis=0)
    down_weight_raw = contract_rows(activated, signal_low)
    grad_act = times_transposed(signal_low, down_weight)
    unused_value, gelu_pull = jax.vjp(partial(jax.nn.gelu, approximate=True), pre_act)
    grad_pre = gelu_pull(grad_act)[0].astype(jnp.bfloat16)
    up_bias_raw = jnp.sum(grad_pre.astype(jnp.float32), axis=0)
    up_weight_raw = contract_rows(mlp_normed, grad_pre)
    grad_mlp_normed = lax.psum(times_transposed(grad_pre, up_weight), "head")
    grad_after, mlp_gain_raw, mlp_shift_raw = normalize_back(
        grad_mlp_normed, mlp_normal, mlp_inverse, norm_gains[1]
    )
    upper = signal + grad_after
    upper_low = upper.astype(jnp.bfloat16)
    out_bias_raw = jnp.sum(upper, axis=0)
    out_weight_raw = contract_rows(mixed, upper_low)
    grad_mixed = times_transposed(upper_low, out_weight).astype(jnp.bfloat16).reshape(head_shape)
    queries = projected[0].reshape(head_shape)
    keys_local = projected[1].reshape(head_shape)
    values_local = projected[2].reshape(head_shape)
    scores = (
        jnp.einsum("bqhd,bkhd->bhqk", queries, keys_local, preferred_element_type=jnp.float32)
        * score_scale
    )
    probs = jnp.exp(scores - log_total)
    probs_low = probs.astype(jnp.bfloat16)
    grad_probs = jnp.einsum(
        "bqhd,bkhd->bhqk", grad_mixed, values_local, preferred_element_type=jnp.float32
    )
    grad_values = jnp.einsum(
        "bhqk,bqhd->bkhd", probs_low, grad_mixed, preferred_element_type=jnp.float32
    )
    inner_sum = jnp.sum(probs * grad_probs, axis=-1, keepdims=True)
    grad_scores = (probs * (grad_probs - inner_sum) * score_scale).astype(jnp.bfloat16)
    grad_queries = jnp.einsum(
        "bhqk,bkhd->bqhd", grad_scores, keys_local, preferred_element_type=jnp.float32
    )
    grad_keys = jnp.einsum(
        "bhqk,bqhd->bkhd", grad_scores, queries, preferred_element_type=jnp.float32
    )
    grad_project = (
        jnp.stack([grad_queries, grad_keys, grad_values])
        .reshape(3, row_count, local_width)
        .astype(jnp.bfloat16)
    )
    qkv_weight_raw = jnp.einsum(
        "td,ntc->ndc", attn_normed, grad_project, preferred_element_type=jnp.float32
    )
    column_sums = jnp.sum(grad_project.astype(jnp.float32), axis=1)
    qv_bias_raw = jnp.stack([column_sums[0], column_sums[2]])
    grad_attn_normed = lax.psum(
        jnp.einsum("ntc,ndc->td", grad_project, qkv_weight, preferred_element_type=jnp.float32),
        "head",
    )
    grad_start, attn_gain_raw, attn_shift_raw = normalize_back(
        grad_attn_normed, attn_normal, attn_inverse, norm_gains[0]
    )
    lower = upper + grad_start
    mask_embed_raw = jnp.sum(lower * mask_col, axis=0)
    tokens_raw = lower * (1.0 - mask_col)
    gains_raw = jnp.stack([attn_gain_raw, mlp_gain_raw])
    shifts_raw = jnp.stack([attn_shift_raw, mlp_shift_raw])
    biases_raw = jnp.stack([out_bias_raw, down_bias_raw])
    summed = lax.psum(
        (
            mask_embed_raw,
            gains_raw,
            shifts_raw,
            qkv_weight_raw,
            qv_bias_raw,
            out_weight_raw,
            biases_raw,
            up_weight_raw,
            up_bias_raw,
            down_weight_raw,
        ),
        "img",
    )
    loss_scale = lax.axis_size("img") * row_count / masked_sum
    out = result.astype(jnp.bfloat16).reshape(images, seq_len, model_width)
    tokens_grad = (tokens_raw * loss_scale).reshape(images, seq_len, model_width)
    return (
        out,
        tokens_grad,
        summed[0] * loss_scale,
        summed[1] * loss_scale,
        summed[2] * loss_scale,
        summed[3] * loss_scale,
        summed[4] * loss_scale,
        summed[5] * loss_scale,
        summed[6] * loss_scale,
        summed[7] * loss_scale,
        summed[8] * loss_scale,
        summed[9] * loss_scale,
    )


def solution(mesh):
    return jax.shard_map(
        per_device,
        mesh=mesh,
        in_specs=(
            P("img", None, None),
            P(),
            P(),
            P(),
            P(None, None, "head"),
            P(None, "head"),
            P("head", None),
            P(),
            P(None, "head"),
            P("head"),
            P("head", None),
            P("img"),
            P("img", None),
            P("img", None, None),
        ),
        out_specs=(
            P("img", None, None),
            P("img", None, None),
            P(),
            P(),
            P(),
            P(None, None, "head"),
            P(None, "head"),
            P("head", None),
            P(),
            P(None, "head"),
            P("head"),
            P("head", None),
        ),
        check_vma=False,
    )
```

profile of v0, /device:TPU:0, one launch (start us, length us, event | category | flops | bytes accessed | tf_op | source)
XLA Modules:
  0.0 1022.0 jit_solution(18225187835026592122)
XLA Ops:
  23.9 5.7 fusion.141
  36.3 149.1 %all-reduce.9.cloned.1.call-done = f32[1280,768]{1,0:T(8,128)} async-done(((f32[1280,768]{1,0:T(8,128)}), f32[1280,768]{1,0:T(8,128)}) %all-reduce.9.cloned.1.call-update) | async-done | bytes 3932176 | tf_op jit(solution)/shard_map/psum | solution.py:83
  191.1 7.2 fusion.89
  198.3 145.6 %all-reduce.11.cloned.1.call-done = f32[1280,768]{1,0:T(8,128)} async-done(((f32[1280,768]{1,0:T(8,128)}), f32[1280,768]{1,0:T(8,128)}) %all-reduce.11.cloned.1.call-update) | async-done | bytes 3932176 | tf_op jit(solution)/shard_map/psum | solution.py:89
  343.9 5.1 add_add_fusion.1
  373.4 3.7 fusion.153
  377.1 140.0 %all-reduce.13.cloned.1.call-done = f32[1280,768]{1,0:T(8,128)} async-done(((f32[1280,768]{1,0:T(8,128)}), f32[1280,768]{1,0:T(8,128)}) %all-reduce.13.cloned.1.call-update) | async-done | bytes 3932176 | tf_op jit(solution)/shard_map/psum | solution.py:83
  517.1 3.8 fusion.135
  524.5 6.0 convert_reduce_fusion
  531.7 3.7 fusion.154
  535.8 145.2 %all-reduce.15.cloned.1.call-done = f32[1280,768]{1,0:T(8,128)} async-done(((f32[1280,768]{1,0:T(8,128)}), f32[1280,768]{1,0:T(8,128)}) %all-reduce.15.cloned.1.call-update) | async-done | bytes 3932176 | tf_op jit(solution)/shard_map/psum | solution.py:171
  681.0 4.7 multiply_reduce_fusion.4
  693.4 4.4 fusion.94
  697.7 4.3 fusion.76
  702.1 10.6 %fusion.82 = bf16[5,256,4,48]{1,3,2,0:T(8,128)(2,1)} fusion(f32[5,4,256,256]{2,3,1,0:T(8,128)} %fusion.94, f32[5,4,256,256]{2,3,1,0:T(8,128)} %copy-done.10, f32[5,4,256]{2,1,0:T(4,128)S(1)} %log_add_fusion, bf16[5,256,4,48]{1,0,3,2:T(8,128)(2,1)} %copy-done.23), kind=kOutput, calls=%fused_computation.104 | convolution fusion | flops 137876736 | bytes 11489280 | tf_op jit(solution)/shard_map/bhqk,bkhd->bqhd/dot_general | solution.py:197
  712.7 9.4 fusion.79
  734.4 4.8 convolution_bitcast_fusion
  739.3 6.4 fusion.131
  745.8 3.5 fusion.58
  757.0 127.9 %all-reduce.17.cloned.1.call-done = f32[1280,768]{1,0:T(8,128)} async-done(((f32[1280,768]{1,0:T(8,128)}), f32[1280,768]{1,0:T(8,128)}) %all-reduce.17.cloned.1.call-update) | async-done | bytes 3932176 | tf_op jit(solution)/shard_map/psum | solution.py:213
  884.9 5.2 multiply_reduce_fusion.5
  890.5 4.7 multiply_reduce_fusion.6
  895.2 26.4 %all-reduce = (f32[]{:T(128)}, f32[768]{0:T(1024)S(1)}, f32[2,768]{1,0:T(2,128)S(1)}, f32[2,768]{1,0:T(2,128)S(1)}, f32[2,192]{1,0:T(2,128)S(1)}, /*index=5*/f32[2,768]{1,0:T(2,128)S(1)}, f32[768]{0:T(1024)S(1)}) all-reduce(f32[]{:T(128)} %convert_reduce_fusion.2, ...), channel_id=1, replica_groups=mesh['img'=8,'head'=4] {'img'}, use_global_device_ids=true, to_apply=%region_23.24 | all-reduce | flops 6529 | bytes 52232 | tf_op jit(solution)/shard_map/psum | solution.py:129
  922.3 79.6 %all-reduce.19.cloned.1.call-done = (f32[3,768,192]{1,2,0:T(8,128)}, f32[192,768]{1,0:T(8,128)}, f32[768,768]{1,0:T(8,128)}, f32[768,768]{1,0:T(8,128)}) async-done(((f32[3,768,192]{1,2,0:T(8,128)}, f32[192,768]{1,0:T(8,128)}, f32[768,768]{1,0:T(8,128)}, f32[768,768]{1,0:T(8,128)}), (f32[3,768,192]{1,2,0:T(8,128)}, f32[192,768]{1,0:T(8,128)}, f32[768,768]{1,0:T(8,128)}, ...) | async-done | bytes 7077904 | tf_op jit(solution)/shard_map/psum | solution.py:226
  (197 shorter events, 99.3 us)
Async XLA Ops:
  7.2 183.9 %copy-start = (bf16[768,768]{1,0:T(8,128)(2,1)S(1)}, bf16[768,768]{1,0:T(8,128)(2,1)}, u32[]{:S(2)}) copy-start(bf16[768,768]{1,0:T(8,128)(2,1)} %param.22) | copy-start | bytes 3538948
  7.2 5.5 copy-start.31
  7.2 5.5 copy-start.12
  7.2 5.5 copy-start.35
  7.2 178.2 %all-reduce.9.cloned.1.call-start = ((), (), s32[]{:S(2)}) async-start(), calls=%async_computation | async-start | bytes 7864320 | tf_op jit(solution)/shard_map/psum | solution.py:83
  29.6 3.8 copy-start.18
  36.1 307.8 %all-reduce.11.cloned.1.call-start = ((), (), s32[]{:S(2)}) async-start(), calls=%async_computation.1 | async-start | bytes 7864320 | tf_op jit(solution)/shard_map/psum | solution.py:89
  198.3 318.8 %all-reduce.13.cloned.1.call-start = ((), (), s32[]{:S(2)}) async-start(), calls=%async_computation.2 | async-start | bytes 7864320 | tf_op jit(solution)/shard_map/psum | solution.py:83
  358.7 7.6 copy-start.22
  360.6 5.7 copy-start.23
  371.4 309.6 %all-reduce.15.cloned.1.call-start = ((), (), s32[]{:S(2)}) async-start(), calls=%async_computation.3 | async-start | bytes 7864320 | tf_op jit(solution)/shard_map/psum | solution.py:171
  520.9 9.5 copy-start.8
  520.9 3.5 copy-start.42
  535.4 349.5 %all-reduce.17.cloned.1.call-start = ((), (), s32[]{:S(2)}) async-start(), calls=%async_computation.4 | async-start | bytes 7864320 | tf_op jit(solution)/shard_map/psum | solution.py:213
  681.0 4.7 copy-start.9
  681.0 5.6 copy-start.15
  702.1 10.6 %copy-start.24 = (bf16[5,256,4,48]{1,0,3,2:T(8,128)(2,1)S(1)}, bf16[5,256,4,48]{1,0,3,2:T(8,128)(2,1)}, u32[]{:S(2)}) copy-start(bf16[5,256,4,48]{1,0,3,2:T(8,128)(2,1)} %reshape_squeeze.25) | copy-start | bytes 1474564
  739.3 262.6 %all-reduce.19.cloned.1.call-start = ((), (), s32[]{:S(2)}) async-start(), calls=%async_computation.5 | async-start | bytes 14155776 | tf_op jit(solution)/shard_map/psum | solution.py:226
  739.3 6.5 copy-start.28
  739.3 6.5 copy-start.43
  884.9 5.3 copy-start.4
  884.9 5.6 copy-start.7
  1001.9 4.9 copy-start.30
  1005.2 7.3 copy-start.14
  (27 other events, 57.9 us)
Sparse Core Ops, SparseCore 0:
  36.2 149.2 all-reduce.8
  198.4 145.4 all-reduce.10
  371.6 145.4 all-reduce.12
  535.5 145.4 all-reduce.14
  739.4 145.4 all-reduce.16
  889.6 112.2 all-reduce.18
where the time goes:
time: 1030 us; the launch traced here: 1020 us
  waiting for transfers between devices  787 us (76%)
  matrix products  90.1 us (9%)
  other arithmetic  58.6 us (6%)
  local copies, waits for them, and re-layouts  42.6 us (4%)
  blocking collectives  26.4 us (3%)
  between operations  15.8 us (2%)
    psum x2, waiting for transfers between devices, forward(): lax.psum(jnp.dot(mixed, out_weight, preferred_element_type=jnp.float32),...  289 us
    psum x1, waiting for transfers between devices, forward(): lax.psum(jnp.dot(activated, down_weight, preferred_element_type=jnp.float...  146 us
    psum x1, waiting for transfers between devices, per_device(): grad_mlp_normed = lax.psum(times_transposed(grad_pre, up_weight), 'head')  145 us
    psum x1, waiting for transfers between devices, per_device(): lax.psum(jnp.einsum('ntc,ndc->td', grad_project, qkv_weight, preferred_el...  128 us
    psum x1, waiting for transfers between devices, per_device(): lax.psum((mask_embed_raw, gains_raw, shifts_raw, qkv_weight_raw, qv_bias_...  79.6 us
    psum x1, blocking collectives, per_device(): masked_sum = lax.psum(local_count, 'img')  26.4 us
  transfers between devices with their start and end apart: 6, of which 6 were waited for; matrix products, arithmetic and copies ran while one was open for 3% of the time, Pallas kernels for 0%

commit v1 on v0

--- a/solution.py
+++ b/solution.py
@@ -38,6 +38,10 @@
 
 
 def forward(start, params, images, seq_len):
+
+    def _produce_slots(xs):
+        return jnp.sum(lax.all_gather(xs, "head"), axis=0)
+
     (
         norm_gains,
         norm_shifts,
@@ -86,7 +90,7 @@
     mlp_normed = mlp_normed.astype(jnp.bfloat16)
     pre_act = jnp.dot(mlp_normed, up_weight, preferred_element_type=jnp.float32) + up_bias
     activated = jax.nn.gelu(pre_act, approximate=True).astype(jnp.bfloat16)
-    branch = lax.psum(jnp.dot(activated, down_weight, preferred_element_type=jnp.float32), "head")
+    branch = _produce_slots(jnp.dot(activated, down_weight, preferred_element_type=jnp.float32))
     after_mlp = after_attn + branch + output_biases[1]
     saved = (
         attn_normal,

time: 1030 us -> 1170 us (1.14)
  waiting for transfers between devices: 787 us -> 897 us
    all_gather x0 -> x1, waiting for transfers between devices: none -> 269 us  [_produce_slots(): return jnp.sum(lax.all_gather(xs, 'head'), axis=0)]
    psum x1 -> x0, waiting for transfers between devices: 146 us -> none  [forward(): lax.psum(jnp.dot(activated, down_weight, preferred_element_type=jnp.float...]
    psum x2, waiting for transfers between devices: 289 us -> 276 us  [forward(): lax.psum(jnp.dot(mixed, out_weight, preferred_element_type=jnp.float32),...]
    psum x1, starting transfers between devices: 0.25 us -> 12.2 us  [per_device(): grad_mlp_normed = lax.psum(times_transposed(grad_pre, up_weight), 'head')]
where the time goes in v1:
time: 1170 us; the launch traced here: 1160 us
  waiting for transfers between devices  897 us (77%)
  matrix products  92.3 us (8%)
  other arithmetic  68 us (6%)
  local copies, waits for them, and re-layouts  50.5 us (4%)
  blocking collectives  26.4 us (2%)
  between operations  16 us (1%)
  starting transfers between devices  12.7 us (1%)
    psum x2, waiting for transfers between devices, forward(): lax.psum(jnp.dot(mixed, out_weight, preferred_element_type=jnp.float32),...  276 us
    all_gather x1, waiting for transfers between devices, _produce_slots(): return jnp.sum(lax.all_gather(xs, 'head'), axis=0)  269 us
    psum x1, waiting for transfers between devices, per_device(): grad_mlp_normed = lax.psum(times_transposed(grad_pre, up_weight), 'head')  146 us
    psum x1, waiting for transfers between devices, per_device(): lax.psum(jnp.einsum('ntc,ndc->td', grad_project, qkv_weight, preferred_el...  127 us
    psum x1, waiting for transfers between devices, per_device(): lax.psum((mask_embed_raw, gains_raw, shifts_raw, qkv_weight_raw, qv_bias_...  79.6 us
    psum x1, blocking collectives, per_device(): masked_sum = lax.psum(local_count, 'img')  26.4 us
  transfers between devices with their start and end apart: 6, of which 6 were waited for; matrix products, arithmetic and copies ran while one was open for 3% of the time, Pallas kernels for 0%

profile of v1, /device:TPU:0, one launch (start us, length us, event | category | flops | bytes accessed | tf_op | source)
XLA Modules:
  0.0 1162.8 jit_solution(15082226573791682832)
XLA Ops:
  24.5 5.7 fusion.141
  37.0 149.0 %all-reduce.8.cloned.1.call-done = f32[1280,768]{1,0:T(8,128)} async-done(((f32[1280,768]{1,0:T(8,128)}), f32[1280,768]{1,0:T(8,128)}) %all-reduce.8.cloned.1.call-update) | async-done | bytes 3932176 | tf_op jit(solution)/shard_map/psum | solution.py:87
  191.7 7.2 fusion.89
  198.9 268.7 %all-gather.3.cloned.1.call-done = f32[5120,768]{1,0:T(8,128)} async-done(((f32[1280,768]{1,0:T(8,128)}), f32[5120,768]{1,0:T(8,128)}) %all-gather.3.cloned.1.call-update) | async-done | bytes 15728656 | tf_op jit(solution)/shard_map/all_gather | solution.py:43
  467.6 8.9 reduce_sum.239
  476.6 5.1 add_add_fusion.1
  504.1 12.2 %all-reduce.12.cloned.1.call-start = ((), (), s32[]{:S(2)}) async-start(), calls=%async_computation.2 | async-start | bytes 7864320 | tf_op jit(solution)/shard_map/psum | solution.py:175
  518.0 3.7 fusion.153
  521.7 127.2 %all-reduce.10.cloned.1.call-done = f32[1280,768]{1,0:T(8,128)} async-done(((f32[1280,768]{1,0:T(8,128)}), f32[1280,768]{1,0:T(8,128)}) %all-reduce.10.cloned.1.call-update) | async-done | bytes 3932176 | tf_op jit(solution)/shard_map/psum | solution.py:87
  648.9 3.8 fusion.135
  656.3 6.5 convert_reduce_fusion
  667.8 145.6 %all-reduce.12.cloned.1.call-done = f32[1280,768]{1,0:T(8,128)} async-done(((f32[1280,768]{1,0:T(8,128)}), f32[1280,768]{1,0:T(8,128)}) %all-reduce.12.cloned.1.call-update) | async-done | bytes 3932176 | tf_op jit(solution)/shard_map/psum | solution.py:175
  813.4 4.9 multiply_reduce_fusion.4
  826.5 4.8 fusion.94
  831.2 4.4 fusion.76
  835.6 10.7 fusion.82
  846.3 10.7 fusion.79
  875.1 4.8 convolution_bitcast_fusion
  880.6 6.4 fusion.131
  898.8 126.8 %all-reduce.14.cloned.1.call-done = f32[1280,768]{1,0:T(8,128)} async-done(((f32[1280,768]{1,0:T(8,128)}), f32[1280,768]{1,0:T(8,128)}) %all-reduce.14.cloned.1.call-update) | async-done | bytes 3932176 | tf_op jit(solution)/shard_map/psum | solution.py:217
  1025.6 4.9 multiply_reduce_fusion.5
  1031.2 4.7 multiply_reduce_fusion.6
  1035.9 26.4 %all-reduce = (f32[]{:T(128)}, f32[768]{0:T(1024)S(1)}, f32[2,768]{1,0:T(2,128)S(1)}, f32[2,768]{1,0:T(2,128)S(1)}, f32[2,192]{1,0:T(2,128)S(1)}, /*index=5*/f32[2,768]{1,0:T(2,128)S(1)}, f32[768]{0:T(1024)S(1)}) all-reduce(f32[]{:T(128)} %convert_reduce_fusion.2, ...), channel_id=1, replica_groups=mesh['img'=8,'head'=4] {'img'}, use_global_device_ids=true, to_apply=%region_23.24 | all-reduce | flops 6529 | bytes 52232 | tf_op jit(solution)/shard_map/psum | solution.py:133
  1063.0 79.6 %all-reduce.16.cloned.1.call-done = (f32[3,768,192]{1,2,0:T(8,128)}, f32[192,768]{1,0:T(8,128)}, f32[768,768]{1,0:T(8,128)}, f32[768,768]{1,0:T(8,128)}) async-done(((f32[3,768,192]{1,2,0:T(8,128)}, f32[192,768]{1,0:T(8,128)}, f32[768,768]{1,0:T(8,128)}, f32[768,768]{1,0:T(8,128)}), (f32[3,768,192]{1,2,0:T(8,128)}, f32[192,768]{1,0:T(8,128)}, f32[768,768]{1,0:T(8,128)}, ...) | async-done | bytes 7077904 | tf_op jit(solution)/shard_map/psum | solution.py:230
  (204 shorter events, 114.3 us)
Async XLA Ops:
  7.2 184.5 %copy-start = (bf16[768,768]{1,0:T(8,128)(2,1)S(1)}, bf16[768,768]{1,0:T(8,128)(2,1)}, u32[]{:S(2)}) copy-start(bf16[768,768]{1,0:T(8,128)(2,1)} %param.22) | copy-start | bytes 3538948
  7.2 6.1 copy-start.30
  7.2 6.1 copy-start.11
  7.2 6.1 copy-start.38
  7.2 178.8 %all-reduce.8.cloned.1.call-start = ((), (), s32[]{:S(2)}) async-start(), calls=%async_computation | async-start | bytes 7864320 | tf_op jit(solution)/shard_map/psum | solution.py:87
  13.9 639.5 %copy-start.35 = (f32[768]{0:T(1024)}, f32[768]{0:T(1024)S(1)}, u32[]{:S(2)}) copy-start(f32[768]{0:T(1024)S(1)} %get-tuple-element.26) | copy-start | bytes 9220
  36.7 431.0 %all-gather.3.cloned.1.call-start = ((), (), s32[]{:S(2)}) async-start(), calls=%async_computation.4 | async-start | bytes 19660800 | tf_op jit(solution)/shard_map/all_gather | solution.py:43
  198.9 450.0 %all-reduce.10.cloned.1.call-start = ((), (), s32[]{:S(2)}) async-start(), calls=%async_computation.1 | async-start | bytes 7864320 | tf_op jit(solution)/shard_map/psum | solution.py:87
  491.3 7.6 copy-start.22
  493.2 5.7 copy-start.23
  501.4 14.9 %copy-start.12 = (bf16[5,256,768]{2,1,0:T(8,128)(2,1)S(1)}, bf16[5,256,768]{2,1,0:T(8,128)(2,1)}, u32[]{:S(2)}) copy-start(bf16[5,256,768]{2,1,0:T(8,128)(2,1)} %param.27) | copy-start | bytes 5898244
  504.1 309.3 %all-reduce.12.cloned.1.call-start = ((), (), s32[]{:S(2)}) async-start(), calls=%async_computation.2 | async-start | bytes 7864320 | tf_op jit(solution)/shard_map/psum | solution.py:175
  652.8 10.0 copy-start.7
  667.8 357.8 %all-reduce.14.cloned.1.call-start = ((), (), s32[]{:S(2)}) async-start(), calls=%async_computation.3 | async-start | bytes 7864320 | tf_op jit(solution)/shard_map/psum | solution.py:217
  813.4 5.0 copy-start.8
  813.4 5.6 copy-start.14
  826.5 4.8 copy-start.17
  880.0 262.6 %all-reduce.16.cloned.1.call-start = ((), (), s32[]{:S(2)}) async-start(), calls=%async_computation.5 | async-start | bytes 14155776 | tf_op jit(solution)/shard_map/psum | solution.py:230
  880.6 6.4 copy-start.27
  880.6 6.4 copy-start.46
  1025.6 5.0 copy-start.3
  1025.6 5.6 copy-start.6
  1142.6 4.9 copy-start.29
  1146.0 7.3 copy-start.13
  (30 other events, 66.7 us)
Sparse Core Ops, SparseCore 0:
  36.8 149.2 all-reduce.7
  199.0 268.5 all-gather.2
  504.2 144.6 all-reduce.9
  667.9 145.4 all-reduce.11
  880.1 145.4 all-reduce.13
  1030.3 112.2 all-reduce.15
